TPU v7x, 512 devices: a whole 4x8x8 slice. The times are simulated.
512 devices in a mesh: gz: 32 (over z_hi, x, core), gy: 16 (over z_lo, y).
Axes of the slice: x: 4, y: 8, z: 8 (z_hi: 4, z_lo: 2; z = z_hi * 2 + z_lo), core: 2. Of those that a mesh axis runs over, the one named last changes fastest.
Arguments:
- filtered: bfloat16 [16, 256, 4096], P(None, 'gz', 'gy'), may hold values from -6 to 6
- angle_index: int32 [16], replicated, may hold values from 0 to 3599
- band_offset: int32 [16, 32], P(None, 'gz'), may hold values from 0 to 12, as said below
- band_length: int32 [16, 32], P(None, 'gz'), may hold values from 4 to 12
- foot_block: int32 [16, 64, 64], P(None, 'gy'), may hold values from 0 to 62, as said below
Outputs:
- denoised: float32 [64, 256, 4096], P('gy', 'gz')
Inputs may be any that keep to these rules, and one draw needn't show every extreme that they name: band_offset + band_length <= 16 for every projection and group. foot_block[p, y, b] is b plus a shift of -2 to 2 that depends only on p and y, clipped to the range.
All inputs are finite; a program needn't handle non-finite values.
Results may differ from a plain program's by a relative error of at most 0.0041.
Values may be sent and summed in bfloat16 or wider, within the bound.
A program may use at most 64 MiB of HBM per device.

v0:
```python
import math
import jax
import jax.numpy as jnp
from jax import lax
from jax.sharding import PartitionSpec as P

X = 4096
P_SIZE = 16
NANG = 3600
BLOCK = 64
ITERS = 2
step_length = 0.25
smooth_weight = 0.3
gradient_floor = 0.01
shift_reach = 8.0


def with_halo(cells, sides, width):
    for axis, dim in sides:
        count = lax.axis_size(axis)
        ends = count - 1
        head = lax.slice_in_dim(cells, 0, width, axis=dim)
        tail = lax.slice_in_dim(cells, cells.shape[dim] - width, cells.shape[dim], axis=dim)
        cells = jnp.concatenate(
            [
                lax.ppermute(tail, axis, [(i, (i + 1) % count) for i in range(ends)]),
                cells,
                lax.ppermute(head, axis, [((i + 1) % count, i) for i in range(ends)]),
            ],
            axis=dim,
        )
    return cells


def geometry(angle_value):
    radians = 2.0 * math.pi * angle_value.astype(jnp.float32) / NANG
    stretch = 0.5 + 0.5 * jnp.abs(jnp.cos(radians))
    spread = 1.0 + jnp.abs(jnp.sin(radians))
    return (radians, stretch, spread)


def footprint(radians, stretch, spread, row_global, rows_total, block_size):
    shifted = shift_reach * jnp.sin(radians + 2.0 * math.pi * row_global / rows_total)
    inside = jnp.arange(block_size).astype(jnp.float32) - 0.5 * (block_size - 1)
    centre = block_size + inside[None, :] * stretch + shifted[:, None]
    places = jnp.arange(2 * block_size).astype(jnp.float32) + 0.5
    weights = (
        jnp.maximum(0.0, 1.0 - jnp.abs(places[None, None, :] - centre[:, :, None]) / spread)
        / spread
    )
    return weights.astype(jnp.bfloat16)


def axial_table(offsets, lengths, depth_count):
    offset_real = offsets.astype(jnp.float32)[..., None]
    length_real = lengths.astype(jnp.float32)[..., None]
    depth_place = jnp.arange(depth_count).astype(jnp.float32) + 0.5
    centre = offset_real + depth_place * length_real / depth_count
    row_number = jnp.arange(2 * depth_count)
    row_place = row_number.astype(jnp.float32) + 0.5
    triangle = jnp.maximum(0.0, 1.0 - jnp.abs(row_place - centre[..., None]))
    inside = (row_number >= offsets[..., None, None]) & (
        row_number < (offsets + lengths)[..., None, None]
    )
    return jnp.where(inside, triangle, 0.0).astype(jnp.bfloat16)


def smooth_update(current, fidelity, row_first, depth_first, rows_total, depth_total):
    row_index = row_first + jnp.arange(current.shape[0])
    depth_index = depth_first + jnp.arange(current.shape[1])
    keep_rows = ((row_index >= 0) & (row_index < rows_total - 1)).astype(jnp.float32)[:, None, None]
    keep_depth = ((depth_index >= 0) & (depth_index < depth_total - 1)).astype(jnp.float32)[
        None, :, None
    ]
    forward_rows = (
        jnp.concatenate([current[1:] - current[:-1], jnp.zeros_like(current[:1])], 0) * keep_rows
    )
    forward_depth = (
        jnp.concatenate([current[:, 1:] - current[:, :-1], jnp.zeros_like(current[:, :1])], 1)
        * keep_depth
    )
    forward_width = jnp.concatenate(
        [current[:, :, 1:] - current[:, :, :-1], jnp.zeros_like(current[:, :, :1])], 2
    )
    magnitude = jnp.sqrt(
        forward_rows * forward_rows
        + forward_depth * forward_depth
        + forward_width * forward_width
        + gradient_floor
    )
    normal_rows = forward_rows / magnitude
    normal_depth = forward_depth / magnitude
    normal_width = forward_width / magnitude
    divergence = normal_rows - jnp.concatenate(
        [jnp.zeros_like(normal_rows[:1]), normal_rows[:-1]], 0
    )
    divergence = (
        divergence
        + normal_depth
        - jnp.concatenate([jnp.zeros_like(normal_depth[:, :1]), normal_depth[:, :-1]], 1)
    )
    divergence = (
        divergence
        + normal_width
        - jnp.concatenate([jnp.zeros_like(normal_width[:, :, :1]), normal_width[:, :, :-1]], 2)
    )
    return current + step_length * (smooth_weight * divergence - (current - fidelity))


def per_device(filtered, angle_index, band_offset, band_length, foot_block):
    depth_count = filtered.shape[1]
    row_count = foot_block.shape[1]
    extended_band = with_halo(filtered, (("gz", 1),), depth_count // 2)
    axial_weights = axial_table(band_offset[:, 0], band_length[:, 0], depth_count)
    summed_rows = jnp.einsum(
        "pzv,pvu->pzu",
        axial_weights,
        lax.all_gather(extended_band, "gy", axis=2, tiled=True),
        preferred_element_type=jnp.float32,
    )
    columns = summed_rows.astype(jnp.bfloat16)
    column_count = columns.shape[2]
    row_base = lax.axis_index("gy") * row_count
    depth_base = lax.axis_index("gz") * depth_count
    rows_total = lax.axis_size("gy") * row_count
    depth_total = lax.axis_size("gz") * depth_count
    row_global = (row_base + jnp.arange(row_count)).astype(jnp.float32)

    def one_projection(running, inputs):
        projected, angle_value, blocks = inputs
        radians, stretch, spread = geometry(angle_value)
        weights = footprint(radians, stretch, spread, row_global, rows_total, BLOCK)
        column_tiles = projected.reshape(depth_count, column_count // BLOCK, BLOCK)
        window = jnp.concatenate([column_tiles[:, blocks], column_tiles[:, blocks + 1]], axis=-1)
        product = jnp.einsum("yiu,zybu->yzbi", weights, window, preferred_element_type=jnp.float32)
        return (running + product.reshape(running.shape), None)

    initial = jnp.zeros((row_count, depth_count, X), jnp.float32)
    summed, _unused = lax.scan(one_projection, initial, (columns, angle_index, foot_block))
    backprojection = math.pi / P_SIZE * summed
    current = backprojection
    padded_fidelity = jnp.pad(backprojection, ((1, 1), (1, 1), (0, 0)))
    for turn_index in range(ITERS):
        extended = with_halo(current, (("gz", 1), ("gy", 0)), 1)
        updated = smooth_update(
            extended, padded_fidelity, row_base - 1, depth_base - 1, rows_total, depth_total
        )
        current = updated[1:-1, 1:-1]
    return current


def solution(mesh):
    return jax.shard_map(
        per_device,
        mesh=mesh,
        in_specs=(P(None, "gz", "gy"), P(), P(None, "gz"), P(None, "gz"), P(None, "gy", None)),
        out_specs=P("gy", "gz", None),
        check_vma=False,
    )
```

profile of v0, /device:TPU:191, one launch (start us, length us, event | category | flops | bytes accessed | tf_op | source)
XLA Modules:
  0.0 257.0 jit_solution(1076519616723766050)
XLA Ops:
  6.5 0.9 fusion.37
  7.5 7.5 %collective-permute-start = (bf16[16,4,256]{2,1,0:T(4,128)(2,1)S(1)}, bf16[16,4,256]{2,1,0:T(4,128)(2,1)S(1)}, u32[]{:S(2)}, u32[]{:S(2)}) collective-permute-start(bf16[16,4,256]{2,1,0:T(4,128)(2,1)S(1)} %get-tuple-element.140), channel_id=1, source_target_pairs={{0,16},{16,32},{32,48},{48,64},{64,80},{80,96},{96,112},{112,128},... | collective-permute-start | bytes 98312 | tf_op jit(solution)/shard_map/ppermute | solution.py:26
  15.0 1.9 collective-permute-start.1
  16.9 7.5 %collective-permute-done.1 = bf16[16,4,256]{2,1,0:T(4,128)(2,1)S(1)} collective-permute-done((bf16[16,4,256]{2,1,0:T(4,128)(2,1)S(1)}, bf16[16,4,256]{2,1,0:T(4,128)(2,1)S(1)}, u32[]{:S(2)}, u32[]{:S(2)}) %collective-permute-start.1) | collective-permute-done | bytes 32800 | tf_op jit(solution)/shard_map/ppermute | solution.py:28
  24.4 1.6 pad_maximum_fusion.8
  28.2 60.6 %all-gather.2.cloned.1.call-done = bf16[16,16,4096]{2,1,0:T(8,128)(2,1)} async-done(((bf16[16,16,256]{2,1,0:T(8,128)(2,1)}), bf16[16,16,4096]{2,1,0:T(8,128)(2,1)}) %all-gather.2.cloned.1.call-update) | async-done | bytes 2097168 | tf_op jit(solution)/shard_map/all_gather | solution.py:118
  88.8 2.1 convolution_convert_fusion
  90.9 90.2 %while.13 = (s32[]{:T(128)}, f32[4,8,4096]{2,1,0:T(8,128)S(1)}, bf16[16,8,4096]{2,1,0:T(8,128)(2,1)S(1)}, s32[16,4,64]{2,1,0:T(4,128)}, s32[16]{0:T(128)S(1)}, /...) while((s32[]{:T(128)}, f32[4,8,4096]{2,1,0:T(8,128)S(1)}, ...), condition=%wide.region_1.2_spmd.clone, body=%wide.region_0.1_spmd.clone.sunk | while | flops 35099164 | bytes 6183707 | solution.py:139
  94.5 0.8 gather_fusion
  99.3 0.8 gather_fusion.1
  100.1 0.8 gather_fusion
  105.8 0.8 gather_fusion
  110.6 0.8 gather_fusion.1
  116.2 0.8 gather_fusion.1
  117.0 0.8 gather_fusion
  121.9 0.8 gather_fusion.1
  127.5 0.8 gather_fusion.1
  133.1 0.8 gather_fusion.1
  134.0 0.8 gather_fusion
  138.8 0.8 gather_fusion.1
  139.6 0.8 gather_fusion
  144.4 0.8 gather_fusion.1
  145.2 0.8 gather_fusion
  150.9 0.8 gather_fusion
  155.7 0.8 gather_fusion.1
  161.3 0.8 gather_fusion.1
  162.2 0.8 gather_fusion
  167.0 0.8 gather_fusion.1
  172.6 0.8 gather_fusion.1
  178.2 0.8 gather_fusion.1
  181.3 15.5 %collective-permute-start.2 = (f32[4,1,4096]{2,1,0:T(1,128)S(1)}, f32[4,1,4096]{2,1,0:T(1,128)S(1)}, u32[]{:S(2)}, u32[]{:S(2)}) collective-permute-start(f32[4,1,4096]{2,1,0:T(1,128)S(1)} %get-tuple-element.138), channel_id=1, source_target_pairs={{0,16},{16,32},{32,48},{48,64},{64,80},{80,96},{96,112},{112,128},... | collective-permute-start | bytes 196616 | tf_op jit(solution)/shard_map/ppermute | solution.py:26
  196.9 1.9 collective-permute-start.3
  198.8 8.6 %collective-permute-done.3 = f32[4,1,4096]{2,1,0:T(1,128)S(1)} collective-permute-done((f32[4,1,4096]{2,1,0:T(1,128)S(1)}, f32[4,1,4096]{2,1,0:T(1,128)S(1)}, u32[]{:S(2)}, u32[]{:S(2)}) %collective-permute-start.3) | collective-permute-done | bytes 65568 | tf_op jit(solution)/shard_map/ppermute | solution.py:28
  207.5 1.9 collective-permute-start.4
  209.4 3.4 %collective-permute-start.5 = (f32[1,10,4096]{2,1,0:T(8,128)S(1)}, f32[1,10,4096]{2,1,0:T(8,128)S(1)}, u32[]{:S(2)}, u32[]{:S(2)}) collective-permute-start(f32[1,10,4096]{2,1,0:T(8,128)S(1)} %get-tuple-element.137), channel_id=1, source_target_pairs={{1,0},{2,1},{3,2},{4,3},{5,4},{6,5},{7,6},{8,7},{9,8},{10,9},{11,1... | collective-permute-start | bytes 491528 | tf_op jit(solution)/shard_map/ppermute | solution.py:28
  212.8 1.8 collective-permute-done.4
  214.6 4.0 %collective-permute-done.5 = f32[1,10,4096]{2,1,0:T(8,128)S(1)} collective-permute-done((f32[1,10,4096]{2,1,0:T(8,128)S(1)}, f32[1,10,4096]{2,1,0:T(8,128)S(1)}, u32[]{:S(2)}, u32[]{:S(2)}) %collective-permute-start.5) | collective-permute-done | bytes 163872 | tf_op jit(solution)/shard_map/ppermute | solution.py:28
  219.7 1.1 fusion.19
  221.0 1.2 multiply_add_fusion.1
  222.3 2.9 %collective-permute-start.6 = (f32[4,1,4096]{2,1,0:T(1,128)S(1)}, f32[4,1,4096]{2,1,0:T(1,128)S(1)}, u32[]{:S(2)}, u32[]{:S(2)}) collective-permute-start(f32[4,1,4096]{2,1,0:T(1,128)S(1)} %get-tuple-element.132), channel_id=1, source_target_pairs={{0,16},{16,32},{32,48},{48,64},{64,80},{80,96},{96,112},{112,128},... | collective-permute-start | bytes 196616 | tf_op jit(solution)/shard_map/ppermute | solution.py:26
  225.1 1.9 collective-permute-start.7
  227.1 7.8 %collective-permute-done.7 = f32[4,1,4096]{2,1,0:T(1,128)S(1)} collective-permute-done((f32[4,1,4096]{2,1,0:T(1,128)S(1)}, f32[4,1,4096]{2,1,0:T(1,128)S(1)}, u32[]{:S(2)}, u32[]{:S(2)}) %collective-permute-start.7) | collective-permute-done | bytes 65568 | tf_op jit(solution)/shard_map/ppermute | solution.py:28
  235.0 1.9 collective-permute-start.8
  237.0 3.4 %collective-permute-start.9 = (f32[1,10,4096]{2,1,0:T(8,128)S(1)}, f32[1,10,4096]{2,1,0:T(8,128)S(1)}, u32[]{:S(2)}, u32[]{:S(2)}) collective-permute-start(f32[1,10,4096]{2,1,0:T(8,128)S(1)} %get-tuple-element.135), channel_id=1, source_target_pairs={{1,0},{2,1},{3,2},{4,3},{5,4},{6,5},{7,6},{8,7},{9,8},{10,9},{11,1... | collective-permute-start | bytes 491528 | tf_op jit(solution)/shard_map/ppermute | solution.py:28
  240.3 1.8 collective-permute-done.8
  242.1 4.0 %collective-permute-done.9 = f32[1,10,4096]{2,1,0:T(8,128)S(1)} collective-permute-done((f32[1,10,4096]{2,1,0:T(8,128)S(1)}, f32[1,10,4096]{2,1,0:T(8,128)S(1)}, u32[]{:S(2)}, u32[]{:S(2)}) %collective-permute-start.9) | collective-permute-done | bytes 163872 | tf_op jit(solution)/shard_map/ppermute | solution.py:28
  247.3 1.1 fusion.20
  249.0 1.2 fusion.25
  (315 shorter events, 63.4 us)
Async XLA Ops:
  6.5 82.3 %all-gather.2.cloned.1.call-start = ((), (), s32[]{:S(2)}) async-start(), calls=%async_computation | async-start | bytes 2228224 | tf_op jit(solution)/shard_map/all_gather | solution.py:118
  7.5 9.4 %collective-permute-start = (bf16[16,4,256]{2,1,0:T(4,128)(2,1)S(1)}, bf16[16,4,256]{2,1,0:T(4,128)(2,1)S(1)}, u32[]{:S(2)}, u32[]{:S(2)}) collective-permute-start(bf16[16,4,256]{2,1,0:T(4,128)(2,1)S(1)} %get-tuple-element.140), channel_id=1, source_target_pairs={{0,16},{16,32},{32,48},{48,64},{64,80},{80,96},{96,112},{112,128},... | collective-permute-start | bytes 98312 | tf_op jit(solution)/shard_map/ppermute | solution.py:26
  15.0 9.5 %collective-permute-start.1 = (bf16[16,4,256]{2,1,0:T(4,128)(2,1)S(1)}, bf16[16,4,256]{2,1,0:T(4,128)(2,1)S(1)}, u32[]{:S(2)}, u32[]{:S(2)}) collective-permute-start(bf16[16,4,256]{2,1,0:T(4,128)(2,1)S(1)} %get-tuple-element.141), channel_id=1, source_target_pairs={{16,0},{32,16},{48,32},{64,48},{80,64},{96,80},{112,96},{128,112},... | collective-permute-start | bytes 98312 | tf_op jit(solution)/shard_map/ppermute | solution.py:28
  28.2 62.7 %copy-start = (s32[16]{0:T(128)S(1)}, s32[16]{0:T(128)}, u32[]{:S(2)}) copy-start(s32[16]{0:T(128)} %param.8) | copy-start | bytes 196
  181.3 17.5 %collective-permute-start.2 = (f32[4,1,4096]{2,1,0:T(1,128)S(1)}, f32[4,1,4096]{2,1,0:T(1,128)S(1)}, u32[]{:S(2)}, u32[]{:S(2)}) collective-permute-start(f32[4,1,4096]{2,1,0:T(1,128)S(1)} %get-tuple-element.138), channel_id=1, source_target_pairs={{0,16},{16,32},{32,48},{48,64},{64,80},{80,96},{96,112},{112,128},... | collective-permute-start | bytes 196616 | tf_op jit(solution)/shard_map/ppermute | solution.py:26
  196.9 10.5 %collective-permute-start.3 = (f32[4,1,4096]{2,1,0:T(1,128)S(1)}, f32[4,1,4096]{2,1,0:T(1,128)S(1)}, u32[]{:S(2)}, u32[]{:S(2)}) collective-permute-start(f32[4,1,4096]{2,1,0:T(1,128)S(1)} %get-tuple-element.139), channel_id=1, source_target_pairs={{16,0},{32,16},{48,32},{64,48},{80,64},{96,80},{112,96},{128,112},... | collective-permute-start | bytes 196616 | tf_op jit(solution)/shard_map/ppermute | solution.py:28
  207.5 7.1 %collective-permute-start.4 = (f32[1,10,4096]{2,1,0:T(8,128)S(1)}, f32[1,10,4096]{2,1,0:T(8,128)S(1)}, u32[]{:S(2)}, u32[]{:S(2)}) collective-permute-start(f32[1,10,4096]{2,1,0:T(8,128)S(1)} %get-tuple-element.136), channel_id=1, source_target_pairs={{0,1},{1,2},{2,3},{3,4},{4,5},{5,6},{6,7},{7,8},{8,9},{9,10},{10,1... | collective-permute-start | bytes 491528 | tf_op jit(solution)/shard_map/ppermute | solution.py:26
  209.4 9.2 %collective-permute-start.5 = (f32[1,10,4096]{2,1,0:T(8,128)S(1)}, f32[1,10,4096]{2,1,0:T(8,128)S(1)}, u32[]{:S(2)}, u32[]{:S(2)}) collective-permute-start(f32[1,10,4096]{2,1,0:T(8,128)S(1)} %get-tuple-element.137), channel_id=1, source_target_pairs={{1,0},{2,1},{3,2},{4,3},{5,4},{6,5},{7,6},{8,7},{9,8},{10,9},{11,1... | collective-permute-start | bytes 491528 | tf_op jit(solution)/shard_map/ppermute | solution.py:28
  222.3 4.9 %collective-permute-start.6 = (f32[4,1,4096]{2,1,0:T(1,128)S(1)}, f32[4,1,4096]{2,1,0:T(1,128)S(1)}, u32[]{:S(2)}, u32[]{:S(2)}) collective-permute-start(f32[4,1,4096]{2,1,0:T(1,128)S(1)} %get-tuple-element.132), channel_id=1, source_target_pairs={{0,16},{16,32},{32,48},{48,64},{64,80},{80,96},{96,112},{112,128},... | collective-permute-start | bytes 196616 | tf_op jit(solution)/shard_map/ppermute | solution.py:26
  225.1 9.8 %collective-permute-start.7 = (f32[4,1,4096]{2,1,0:T(1,128)S(1)}, f32[4,1,4096]{2,1,0:T(1,128)S(1)}, u32[]{:S(2)}, u32[]{:S(2)}) collective-permute-start(f32[4,1,4096]{2,1,0:T(1,128)S(1)} %get-tuple-element.133), channel_id=1, source_target_pairs={{16,0},{32,16},{48,32},{64,48},{80,64},{96,80},{112,96},{128,112},... | collective-permute-start | bytes 196616 | tf_op jit(solution)/shard_map/ppermute | solution.py:28
  235.0 7.1 %collective-permute-start.8 = (f32[1,10,4096]{2,1,0:T(8,128)S(1)}, f32[1,10,4096]{2,1,0:T(8,128)S(1)}, u32[]{:S(2)}, u32[]{:S(2)}) collective-permute-start(f32[1,10,4096]{2,1,0:T(8,128)S(1)} %get-tuple-element.134), channel_id=1, source_target_pairs={{0,1},{1,2},{2,3},{3,4},{4,5},{5,6},{6,7},{7,8},{8,9},{9,10},{10,1... | collective-permute-start | bytes 491528 | tf_op jit(solution)/shard_map/ppermute | solution.py:26
  237.0 9.2 %collective-permute-start.9 = (f32[1,10,4096]{2,1,0:T(8,128)S(1)}, f32[1,10,4096]{2,1,0:T(8,128)S(1)}, u32[]{:S(2)}, u32[]{:S(2)}) collective-permute-start(f32[1,10,4096]{2,1,0:T(8,128)S(1)} %get-tuple-element.135), channel_id=1, source_target_pairs={{1,0},{2,1},{3,2},{4,3},{5,4},{6,5},{7,6},{8,7},{9,8},{10,9},{11,1... | collective-permute-start | bytes 491528 | tf_op jit(solution)/shard_map/ppermute | solution.py:28
Sparse Core Ops, SparseCore 0:
  26.1 62.6 all-gather.1
where the time goes:
time: 258 us; the launch traced here: 257 us
  waiting for transfers between devices  96.2 us (37%)
  local copies, waits for them, and re-layouts  54.1 us (21%)
  starting transfers between devices  42.2 us (16%)
  other arithmetic  26.9 us (10%)
  loops' own time  14.3 us (6%)
  between operations  13.7 us (5%)
  matrix products  9.54 us (4%)
    all_gather x1, waiting for transfers between devices, per_device(): lax.all_gather(extended_band, 'gy', axis=2, tiled=True)  60.6 us
    ppermute x5, waiting for transfers between devices, with_halo(): lax.ppermute(head, axis, [((i + 1) % count, i) for i in range(ends)])  32 us
    ppermute x5, starting transfers between devices, with_halo(): lax.ppermute(tail, axis, [(i, (i + 1) % count) for i in range(ends)])  29.7 us
    gather x32, local copies, waits for them, and re-layouts, one_projection(): column_tiles[:, blocks + 1]  17.4 us
    another operation x1, loops' own time, per_device(): lax.scan(one_projection, initial, (columns, angle_index, foot_block))  14.3 us
    gather x16, local copies, waits for them, and re-layouts, one_projection(): column_tiles[:, blocks]  13.1 us
    ppermute x5, starting transfers between devices, with_halo(): lax.ppermute(head, axis, [((i + 1) % count, i) for i in range(ends)])  12.5 us
    select_n x16, other arithmetic, one_projection(): column_tiles[:, blocks]  11 us
  transfers between devices with their start and end apart: 11, of which 8 were waited for; matrix products, arithmetic and copies ran while one was open for 1% of the time, Pallas kernels for 0%

commit v1 on v0

--- a/solution.py
+++ b/solution.py
@@ -13,6 +13,13 @@
 smooth_weight = 0.3
 gradient_floor = 0.01
 shift_reach = 8.0
+
+
+def use_streams(vector, dim_i):
+    extra = jnp.concatenate(
+        lax.all_to_all(jnp.stack([vector for _ in range(lax.psum(1, "gy"))], 0), "gy", 0, 0), dim_i
+    )
+    return extra
 
 
 def with_halo(cells, sides, width):
@@ -115,7 +122,7 @@
     summed_rows = jnp.einsum(
         "pzv,pvu->pzu",
         axial_weights,
-        lax.all_gather(extended_band, "gy", axis=2, tiled=True),
+        use_streams(extended_band, dim_i=2),
         preferred_element_type=jnp.float32,
     )
     columns = summed_rows.astype(jnp.bfloat16)

time: 258 us -> 227 us (0.88)
  waiting for transfers between devices: 96.2 us -> 79.1 us
  between operations: 13.7 us -> 0.35 us
  local copies, waits for them, and re-layouts: 54.1 us -> 58.9 us
  other arithmetic: 26.9 us -> 24.3 us
    all_gather x1 -> x0, waiting for transfers between devices: 60.6 us -> none  [per_device(): lax.all_gather(extended_band, 'gy', axis=2, tiled=True)]
    all_to_all x0 -> x1, waiting for transfers between devices: none -> 42.1 us  [use_streams(): lax.all_to_all(jnp.stack([vector for _ in range(lax.psum(1, 'gy'))], 0),...]
    ppermute x5, starting transfers between devices: 29.7 us -> 21.8 us  [with_halo(): lax.ppermute(tail, axis, [(i, (i + 1) % count) for i in range(ends)])]
    all_to_all x0 -> x1, starting transfers between devices: none -> 7.41 us  [use_streams(): lax.all_to_all(jnp.stack([vector for _ in range(lax.psum(1, 'gy'))], 0),...]
  transfers between devices with their start and end apart: 11 -> 11, of which waited for: 8 -> 8; matrix products, arithmetic and copies ran while one was open for 1% -> 0% of each run, Pallas kernels for 0% -> 0%
where the time goes in v1:
time: 227 us; the launch traced here: 226 us
  waiting for transfers between devices  79.1 us (35%)
  local copies, waits for them, and re-layouts  58.9 us (26%)
  starting transfers between devices  40.2 us (18%)
  other arithmetic  24.3 us (11%)
  loops' own time  15 us (7%)
  matrix products  7.94 us (3%)
    all_to_all x1, waiting for transfers between devices, use_streams(): lax.all_to_all(jnp.stack([vector for _ in range(lax.psum(1, 'gy'))], 0),...  42.1 us
    ppermute x5, waiting for transfers between devices, with_halo(): lax.ppermute(head, axis, [((i + 1) % count, i) for i in range(ends)])  33.6 us
    ppermute x5, starting transfers between devices, with_halo(): lax.ppermute(tail, axis, [(i, (i + 1) % count) for i in range(ends)])  21.8 us
    gather x32, local copies, waits for them, and re-layouts, one_projection(): column_tiles[:, blocks + 1]  17.4 us
    another operation x1, loops' own time, per_device(): lax.scan(one_projection, initial, (columns, angle_index, foot_block))  15 us
    gather x16, local copies, waits for them, and re-layouts, one_projection(): column_tiles[:, blocks]  13.1 us
    ppermute x5, starting transfers between devices, with_halo(): lax.ppermute(head, axis, [((i + 1) % count, i) for i in range(ends)])  11 us
    select_n x16, other arithmetic, one_projection(): column_tiles[:, blocks]  11 us
  transfers between devices with their start and end apart: 11, of which 8 were waited for; matrix products, arithmetic and copies ran while one was open for 0% of the time, Pallas kernels for 0%

profile of v1, /device:TPU:191, one launch (start us, length us, event | category | flops | bytes accessed | tf_op | source)
XLA Modules:
  0.0 225.8 jit_solution(17027110156071805583)
XLA Ops:
  0.0 0.9 fusion.37
  0.9 7.5 %collective-permute-start = (bf16[16,4,256]{2,1,0:T(4,128)(2,1)S(1)}, bf16[16,4,256]{2,1,0:T(4,128)(2,1)S(1)}, u32[]{:S(2)}, u32[]{:S(2)}) collective-permute-start(bf16[16,4,256]{2,1,0:T(4,128)(2,1)S(1)} %get-tuple-element.140), channel_id=1, source_target_pairs={{0,16},{16,32},{32,48},{48,64},{64,80},{80,96},{96,112},{112,128},... | collective-permute-start | bytes 98312 | tf_op jit(solution)/shard_map/ppermute | solution.py:33
  8.4 1.9 collective-permute-start.1
  10.4 7.5 %collective-permute-done.1 = bf16[16,4,256]{2,1,0:T(4,128)(2,1)S(1)} collective-permute-done((bf16[16,4,256]{2,1,0:T(4,128)(2,1)S(1)}, bf16[16,4,256]{2,1,0:T(4,128)(2,1)S(1)}, u32[]{:S(2)}, u32[]{:S(2)}) %collective-permute-start.1) | collective-permute-done | bytes 32800 | tf_op jit(solution)/shard_map/ppermute | solution.py:35
  17.9 0.9 pad_maximum_fusion.8
  18.8 1.5 stack.2
  20.3 7.4 %all-to-all-start = ((bf16[16,16,16,256]{3,2,1,0:T(8,128)(2,1)}), bf16[16,16,16,256]{3,2,1,0:T(8,128)(2,1)}, u32[]{:S(2)}, u32[]{:S(2)}) async-start(bf16[16,16,16,256]{3,2,1,0:T(8,128)(2,1)} %stack.2), calls=%async_computation | async-start | bytes 4194304 | tf_op jit(solution)/shard_map/all_to_all | solution.py:20
  28.0 42.1 %all-to-all-done = bf16[16,16,16,256]{3,2,1,0:T(8,128)(2,1)} async-done(((bf16[16,16,16,256]{3,2,1,0:T(8,128)(2,1)}), bf16[16,16,16,256]{3,2,1,0:T(8,128)(2,1)}, u32[]{:S(2)}, u32[]{:S(2)}) %all-to-all-start) | async-done | bytes 2097184 | tf_op jit(solution)/shard_map/all_to_all | solution.py:20
  70.1 1.8 copy.28
  72.6 92.2 %while.13 = (s32[]{:T(128)}, f32[4,8,4096]{2,1,0:T(8,128)S(1)}, bf16[16,8,4096]{2,1,0:T(8,128)(2,1)S(1)}, s32[16,4,64]{2,1,0:T(4,128)}, s32[16]{0:T(128)S(1)}, /...) while((s32[]{:T(128)}, f32[4,8,4096]{2,1,0:T(8,128)S(1)}, ...), condition=%wide.region_1.2_spmd.clone, body=%wide.region_0.1_spmd.clone.sunk | while | flops 35099164 | bytes 6183707 | solution.py:146
  76.2 0.8 gather_fusion
  81.2 0.8 gather_fusion.1
  82.0 0.8 gather_fusion
  87.7 0.8 gather_fusion
  92.7 0.8 gather_fusion.1
  98.5 0.8 gather_fusion.1
  99.3 0.8 gather_fusion
  104.2 0.8 gather_fusion.1
  110.0 0.8 gather_fusion.1
  115.7 0.8 gather_fusion.1
  116.6 0.8 gather_fusion
  121.5 0.8 gather_fusion.1
  122.3 0.8 gather_fusion
  127.3 0.8 gather_fusion.1
  133.8 0.8 gather_fusion
  138.8 0.8 gather_fusion.1
  145.4 0.8 gather_fusion
  150.3 0.8 gather_fusion.1
  156.1 0.8 gather_fusion.1
  161.8 0.8 gather_fusion.1
  164.9 5.4 %collective-permute-start.2 = (f32[4,1,4096]{2,1,0:T(1,128)S(1)}, f32[4,1,4096]{2,1,0:T(1,128)S(1)}, u32[]{:S(2)}, u32[]{:S(2)}) collective-permute-start(f32[4,1,4096]{2,1,0:T(1,128)S(1)} %get-tuple-element.138), channel_id=1, source_target_pairs={{0,16},{16,32},{32,48},{48,64},{64,80},{80,96},{96,112},{112,128},... | collective-permute-start | bytes 196616 | tf_op jit(solution)/shard_map/ppermute | solution.py:33
  170.4 1.9 collective-permute-start.3
  172.3 7.9 %collective-permute-done.3 = f32[4,1,4096]{2,1,0:T(1,128)S(1)} collective-permute-done((f32[4,1,4096]{2,1,0:T(1,128)S(1)}, f32[4,1,4096]{2,1,0:T(1,128)S(1)}, u32[]{:S(2)}, u32[]{:S(2)}) %collective-permute-start.3) | collective-permute-done | bytes 65568 | tf_op jit(solution)/shard_map/ppermute | solution.py:35
  180.2 3.7 %collective-permute-start.4 = (f32[1,10,4096]{2,1,0:T(8,128)S(1)}, f32[1,10,4096]{2,1,0:T(8,128)S(1)}, u32[]{:S(2)}, u32[]{:S(2)}) collective-permute-start(f32[1,10,4096]{2,1,0:T(8,128)S(1)} %get-tuple-element.136), channel_id=1, source_target_pairs={{0,1},{1,2},{2,3},{3,4},{4,5},{5,6},{6,7},{7,8},{8,9},{9,10},{10,1... | collective-permute-start | bytes 491528 | tf_op jit(solution)/shard_map/ppermute | solution.py:33
  184.0 1.9 collective-permute-start.5
  185.9 1.6 collective-permute-done.4
  187.5 5.7 %collective-permute-done.5 = f32[1,10,4096]{2,1,0:T(8,128)S(1)} collective-permute-done((f32[1,10,4096]{2,1,0:T(8,128)S(1)}, f32[1,10,4096]{2,1,0:T(8,128)S(1)}, u32[]{:S(2)}, u32[]{:S(2)}) %collective-permute-start.5) | collective-permute-done | bytes 163872 | tf_op jit(solution)/shard_map/ppermute | solution.py:35
  194.3 1.1 fusion.19
  195.5 1.2 multiply_add_fusion.1
  196.8 3.2 %collective-permute-start.6 = (f32[4,1,4096]{2,1,0:T(1,128)S(1)}, f32[4,1,4096]{2,1,0:T(1,128)S(1)}, u32[]{:S(2)}, u32[]{:S(2)}) collective-permute-start(f32[4,1,4096]{2,1,0:T(1,128)S(1)} %get-tuple-element.132), channel_id=1, source_target_pairs={{0,16},{16,32},{32,48},{48,64},{64,80},{80,96},{96,112},{112,128},... | collective-permute-start | bytes 196616 | tf_op jit(solution)/shard_map/ppermute | solution.py:33
  200.0 1.9 collective-permute-start.7
  202.1 8.5 %collective-permute-done.7 = f32[4,1,4096]{2,1,0:T(1,128)S(1)} collective-permute-done((f32[4,1,4096]{2,1,0:T(1,128)S(1)}, f32[4,1,4096]{2,1,0:T(1,128)S(1)}, u32[]{:S(2)}, u32[]{:S(2)}) %collective-permute-start.7) | collective-permute-done | bytes 65568 | tf_op jit(solution)/shard_map/ppermute | solution.py:35
  210.7 1.9 collective-permute-start.8
  212.6 3.4 %collective-permute-start.9 = (f32[1,10,4096]{2,1,0:T(8,128)S(1)}, f32[1,10,4096]{2,1,0:T(8,128)S(1)}, u32[]{:S(2)}, u32[]{:S(2)}) collective-permute-start(f32[1,10,4096]{2,1,0:T(8,128)S(1)} %get-tuple-element.135), channel_id=1, source_target_pairs={{1,0},{2,1},{3,2},{4,3},{5,4},{6,5},{7,6},{8,7},{9,8},{10,9},{11,1... | collective-permute-start | bytes 491528 | tf_op jit(solution)/shard_map/ppermute | solution.py:35
  216.0 1.8 collective-permute-done.8
  217.8 4.0 %collective-permute-done.9 = f32[1,10,4096]{2,1,0:T(8,128)S(1)} collective-permute-done((f32[1,10,4096]{2,1,0:T(8,128)S(1)}, f32[1,10,4096]{2,1,0:T(8,128)S(1)}, u32[]{:S(2)}, u32[]{:S(2)}) %collective-permute-start.9) | collective-permute-done | bytes 163872 | tf_op jit(solution)/shard_map/ppermute | solution.py:35
  223.0 1.1 fusion.20
  224.6 1.2 fusion.25
  (320 shorter events, 64.9 us)
Async XLA Ops:
  0.9 9.4 %collective-permute-start = (bf16[16,4,256]{2,1,0:T(4,128)(2,1)S(1)}, bf16[16,4,256]{2,1,0:T(4,128)(2,1)S(1)}, u32[]{:S(2)}, u32[]{:S(2)}) collective-permute-start(bf16[16,4,256]{2,1,0:T(4,128)(2,1)S(1)} %get-tuple-element.140), channel_id=1, source_target_pairs={{0,16},{16,32},{32,48},{48,64},{64,80},{80,96},{96,112},{112,128},... | collective-permute-start | bytes 98312 | tf_op jit(solution)/shard_map/ppermute | solution.py:33
  8.4 9.5 %collective-permute-start.1 = (bf16[16,4,256]{2,1,0:T(4,128)(2,1)S(1)}, bf16[16,4,256]{2,1,0:T(4,128)(2,1)S(1)}, u32[]{:S(2)}, u32[]{:S(2)}) collective-permute-start(bf16[16,4,256]{2,1,0:T(4,128)(2,1)S(1)} %get-tuple-element.141), channel_id=1, source_target_pairs={{16,0},{32,16},{48,32},{64,48},{80,64},{96,80},{112,96},{128,112},... | collective-permute-start | bytes 98312 | tf_op jit(solution)/shard_map/ppermute | solution.py:35
  20.3 7.5 %copy-start = (s32[16,1]{0,1:T(1,128)S(1)}, s32[16,1]{0,1:T(1,128)}, u32[]{:S(2)}) copy-start(s32[16,1]{0,1:T(1,128)} %param.9) | copy-start | bytes 196
  20.3 7.5 %copy-start.1 = (s32[16,1]{0,1:T(1,128)S(1)}, s32[16,1]{0,1:T(1,128)}, u32[]{:S(2)}) copy-start(s32[16,1]{0,1:T(1,128)} %param.10) | copy-start | bytes 196
  20.3 49.7 %all-to-all-start = ((bf16[16,16,16,256]{3,2,1,0:T(8,128)(2,1)}), bf16[16,16,16,256]{3,2,1,0:T(8,128)(2,1)}, u32[]{:S(2)}, u32[]{:S(2)}) async-start(bf16[16,16,16,256]{3,2,1,0:T(8,128)(2,1)} %stack.2), calls=%async_computation | async-start | bytes 4194304 | tf_op jit(solution)/shard_map/all_to_all | solution.py:20
  71.9 0.7 copy-start.2
  164.9 7.4 %collective-permute-start.2 = (f32[4,1,4096]{2,1,0:T(1,128)S(1)}, f32[4,1,4096]{2,1,0:T(1,128)S(1)}, u32[]{:S(2)}, u32[]{:S(2)}) collective-permute-start(f32[4,1,4096]{2,1,0:T(1,128)S(1)} %get-tuple-element.138), channel_id=1, source_target_pairs={{0,16},{16,32},{32,48},{48,64},{64,80},{80,96},{96,112},{112,128},... | collective-permute-start | bytes 196616 | tf_op jit(solution)/shard_map/ppermute | solution.py:33
  170.4 9.8 %collective-permute-start.3 = (f32[4,1,4096]{2,1,0:T(1,128)S(1)}, f32[4,1,4096]{2,1,0:T(1,128)S(1)}, u32[]{:S(2)}, u32[]{:S(2)}) collective-permute-start(f32[4,1,4096]{2,1,0:T(1,128)S(1)} %get-tuple-element.139), channel_id=1, source_target_pairs={{16,0},{32,16},{48,32},{64,48},{80,64},{96,80},{112,96},{128,112},... | collective-permute-start | bytes 196616 | tf_op jit(solution)/shard_map/ppermute | solution.py:35
  180.2 7.3 %collective-permute-start.4 = (f32[1,10,4096]{2,1,0:T(8,128)S(1)}, f32[1,10,4096]{2,1,0:T(8,128)S(1)}, u32[]{:S(2)}, u32[]{:S(2)}) collective-permute-start(f32[1,10,4096]{2,1,0:T(8,128)S(1)} %get-tuple-element.136), channel_id=1, source_target_pairs={{0,1},{1,2},{2,3},{3,4},{4,5},{5,6},{6,7},{7,8},{8,9},{9,10},{10,1... | collective-permute-start | bytes 491528 | tf_op jit(solution)/shard_map/ppermute | solution.py:33
  184.0 9.2 %collective-permute-start.5 = (f32[1,10,4096]{2,1,0:T(8,128)S(1)}, f32[1,10,4096]{2,1,0:T(8,128)S(1)}, u32[]{:S(2)}, u32[]{:S(2)}) collective-permute-start(f32[1,10,4096]{2,1,0:T(8,128)S(1)} %get-tuple-element.137), channel_id=1, source_target_pairs={{1,0},{2,1},{3,2},{4,3},{5,4},{6,5},{7,6},{8,7},{9,8},{10,9},{11,1... | collective-permute-start | bytes 491528 | tf_op jit(solution)/shard_map/ppermute | solution.py:35
  196.8 5.2 %collective-permute-start.6 = (f32[4,1,4096]{2,1,0:T(1,128)S(1)}, f32[4,1,4096]{2,1,0:T(1,128)S(1)}, u32[]{:S(2)}, u32[]{:S(2)}) collective-permute-start(f32[4,1,4096]{2,1,0:T(1,128)S(1)} %get-tuple-element.132), channel_id=1, source_target_pairs={{0,16},{16,32},{32,48},{48,64},{64,80},{80,96},{96,112},{112,128},... | collective-permute-start | bytes 196616 | tf_op jit(solution)/shard_map/ppermute | solution.py:33
  200.0 10.5 %collective-permute-start.7 = (f32[4,1,4096]{2,1,0:T(1,128)S(1)}, f32[4,1,4096]{2,1,0:T(1,128)S(1)}, u32[]{:S(2)}, u32[]{:S(2)}) collective-permute-start(f32[4,1,4096]{2,1,0:T(1,128)S(1)} %get-tuple-element.133), channel_id=1, source_target_pairs={{16,0},{32,16},{48,32},{64,48},{80,64},{96,80},{112,96},{128,112},... | collective-permute-start | bytes 196616 | tf_op jit(solution)/shard_map/ppermute | solution.py:35
  210.7 7.1 %collective-permute-start.8 = (f32[1,10,4096]{2,1,0:T(8,128)S(1)}, f32[1,10,4096]{2,1,0:T(8,128)S(1)}, u32[]{:S(2)}, u32[]{:S(2)}) collective-permute-start(f32[1,10,4096]{2,1,0:T(8,128)S(1)} %get-tuple-element.134), channel_id=1, source_target_pairs={{0,1},{1,2},{2,3},{3,4},{4,5},{5,6},{6,7},{7,8},{8,9},{9,10},{10,1... | collective-permute-start | bytes 491528 | tf_op jit(solution)/shard_map/ppermute | solution.py:33
  212.6 9.2 %collective-permute-start.9 = (f32[1,10,4096]{2,1,0:T(8,128)S(1)}, f32[1,10,4096]{2,1,0:T(8,128)S(1)}, u32[]{:S(2)}, u32[]{:S(2)}) collective-permute-start(f32[1,10,4096]{2,1,0:T(8,128)S(1)} %get-tuple-element.135), channel_id=1, source_target_pairs={{1,0},{2,1},{3,2},{4,3},{5,4},{6,5},{7,6},{8,7},{9,8},{10,9},{11,1... | collective-permute-start | bytes 491528 | tf_op jit(solution)/shard_map/ppermute | solution.py:35
